TPU v7x, 128 devices: a whole 4x4x4 slice. The times are simulated.
128 devices in a mesh: blk: 16 (over z_lo, x, core), narrow: 8 (over z_hi, y).
Axes of the slice: x: 4, y: 4, z: 4 (z_hi: 2, z_lo: 2; z = z_hi * 2 + z_lo), core: 2. Of those that a mesh axis runs over, the one named last changes fastest.
Arguments:
- codes: bfloat16 [24576, 12288], P(('blk', 'narrow')), may hold values from -24 to 24
- signals: bfloat16 [24576, 192], P(('blk', 'narrow')), may hold values from -6 to 6
- dictionary: bfloat16 [12288, 192], P('blk'), may hold values from -0.0546875 to 0.0546875
Outputs:
- new_codes: bfloat16 [24576, 12288], P(('blk', 'narrow'))
- dict_grad: float32 [12288, 192], P(('blk', 'narrow'))
All inputs are finite; a program needn't handle non-finite values.
Results may differ from a plain program's by a relative error of at most 0.0095.
Values may be sent and summed in bfloat16 or wider, within the bound.
No kernel may reach another device: no remote copies, remote signals or barrier semaphores. Data moves between devices by JAX's collectives and lax.ppermute only.
A program may use at most 64 MiB of HBM per device.

v0:
```python
import functools

import jax
import jax.numpy as jnp
from jax import lax
from jax.experimental import pallas as pl
from jax.experimental.pallas import tpu as pltpu
from jax.sharding import Mesh
from jax.sharding import PartitionSpec as P


AXES = ("z_lo", "x", "core", "z_hi", "y")
SIZES = (2, 4, 2, 2, 4)
ANY = pl.BlockSpec(memory_space=pl.ANY)
SMEM = pl.BlockSpec(memory_space=pltpu.SMEM)
VMEM = pl.BlockSpec(memory_space=pltpu.VMEM)
F32, BF16 = jnp.float32, jnp.bfloat16
PARAMS = pltpu.CompilerParams(vmem_limit_bytes=24 << 20)


def near_memory(value):
    return pltpu.with_memory_space_constraint(value, pltpu.VMEM)


def far_memory(value):
    return pltpu.with_memory_space_constraint(value, pltpu.HBM)


def z_step(step):
    def place(z):
        return (z % 2) * 2 + z // 2

    return [(place(z), place((z + step) % 4)) for z in range(4)]


def send_x(value, step):
    return lax.ppermute(value, "x", [(i, (i + step) % 4) for i in range(4)])


def send_z(value, step):
    return lax.ppermute(value, ("z_lo", "z_hi"), z_step(step))


def send_core(value):
    return lax.ppermute(value, "core", [(0, 1), (1, 0)])


def columns(block, width):
    return pl.ds(pl.multiple_of(block * width, 128), width)


def chunk_place(shift, x, z_lo):
    dz, dx = shift
    return ((z_lo[0] + dz) % 2) * 4 + (x[0] + dx) % 4


def halve_kernel(core, x, z_lo, atoms, low, high, sems):
    mid = low.shape[0]
    copies = [
        pltpu.make_async_copy(atoms.at[0:mid], low, sems.at[0]),
        pltpu.make_async_copy(atoms.at[mid : 2 * mid], high, sems.at[1]),
    ]
    for copy in copies:
        copy.start()
    for copy in copies:
        copy.wait()


def halve(core, x, z_lo, atoms):
    piece = pltpu.VMEM((atoms.shape[0] // 2, atoms.shape[1]), BF16)
    return pl.pallas_call(
        halve_kernel,
        out_shape=(piece, piece),
        in_specs=[SMEM, SMEM, SMEM, ANY],
        out_specs=(VMEM, VMEM),
        scratch_shapes=[pltpu.SemaphoreType.DMA((2,))],
        compiler_params=PARAMS,
        name="halve",
    )(core, x, z_lo, far_memory(atoms))


def split_kernel(core, codes, own, away, sems):
    width = own.shape[1] // 8
    copies = []
    for side, (target, half) in enumerate(((away, 1 - core[0]), (own, core[0]))):
        for q in range(8):
            copies.append(
                pltpu.make_async_copy(
                    codes.at[:, columns(2 * q + half, width)],
                    target.at[:, columns(q, width)],
                    sems.at[side, q],
                )
            )
    for copy in copies:
        copy.start()
    for copy in copies:
        copy.wait()


def split(core, codes):
    rows, atom_count = codes.shape
    half = pltpu.VMEM((rows, atom_count // 2), BF16)
    return pl.pallas_call(
        split_kernel,
        out_shape=(half, half),
        in_specs=[SMEM, ANY],
        out_specs=(VMEM, VMEM),
        scratch_shapes=[pltpu.SemaphoreType.DMA((2, 8))],
        compiler_params=PARAMS,
        name="split",
    )(core, far_memory(codes))


def along_atoms(left, right):
    return lax.dot_general(left, right, (((1,), (1,)), ((), ())), preferred_element_type=F32)


def whole(pieces):
    values = [piece[...] for piece in pieces]
    return values[0] if len(values) == 1 else jnp.concatenate(values, axis=0)


def take(refs, counts):
    parts, at = [], 0
    for count in counts:
        parts.append(refs[at : at + count])
        at += count
    return parts, refs[at:]


def estimate_kernel(shifts, counts, has_start, x, z_lo, own, other, *refs):
    start = refs[0] if has_start else None
    parts, rest = take(refs[1:] if has_start else refs, counts)
    (out,) = rest
    rows = own.shape[0]
    width = own.shape[1] // 8
    for k, pieces in enumerate(parts):
        atoms = whole(pieces)
        span = columns(chunk_place(shifts[k], x, z_lo), width)
        for low, source in ((0, own), (rows, other)):
            term = along_atoms(source[:, span], atoms)
            if k:
                out[low : low + rows] += term
            elif has_start:
                out[low : low + rows] = start[low : low + rows] + term
            else:
                out[low : low + rows] = term


def estimate(x, z_lo, own, other, start, shifts, parts):
    rows = own.shape[0]
    features = sum(p.shape[0] for p in parts[0])
    counts = tuple(len(p) for p in parts)
    flat = [p for pieces in parts for p in pieces]
    given = [own, other] + ([] if start is None else [start]) + flat
    return pl.pallas_call(
        functools.partial(estimate_kernel, shifts, counts, start is not None),
        out_shape=pltpu.VMEM((2 * rows, features), F32),
        in_specs=[SMEM, SMEM] + [VMEM] * len(given),
        out_specs=VMEM,
        compiler_params=PARAMS,
        name="estimate",
    )(x, z_lo, *[near_memory(v) for v in given])


def misfit_of(mine, theirs, signal_own, signal_other):
    rows = signal_own.shape[0]
    first = mine[0:rows] + theirs[rows : 2 * rows] - signal_own[...].astype(F32)
    second = mine[rows : 2 * rows] + theirs[0:rows] - signal_other[...].astype(F32)
    return jnp.concatenate([first.astype(BF16), second.astype(BF16)], axis=0)


def update_kernel(shifts, counts, x, z_lo, own, other, mine, theirs, signal_own, signal_other, *refs):
    parts, rest = take(refs, counts)
    fresh_own, fresh_other, out = rest
    rows = own.shape[0]
    width = own.shape[1] // 8
    misfit = misfit_of(mine, theirs, signal_own, signal_other)
    for k, pieces in enumerate(parts):
        atoms = whole(pieces)
        span = columns(chunk_place(shifts[k], x, z_lo), width)
        for low, source, target in ((0, own, fresh_own), (rows, other, fresh_other)):
            correlation = jnp.dot(misfit[low : low + rows], atoms, preferred_element_type=F32)
            value = source[:, span].astype(F32) - 4.0 * correlation
            fresh = (value - jnp.clip(value, -0.5, 0.5)).astype(BF16)
            target[:, span] = fresh
            term = along_atoms(fresh, atoms)
            if k:
                out[low : low + rows] += term
            else:
                out[low : low + rows] = term


def update(x, z_lo, own, other, mine, theirs, signal_own, signal_other, shifts, parts):
    rows = own.shape[0]
    features = sum(p.shape[0] for p in parts[0])
    counts = tuple(len(p) for p in parts)
    flat = [p for pieces in parts for p in pieces]
    given = [own, other, mine, theirs, signal_own, signal_other] + flat
    return pl.pallas_call(
        functools.partial(update_kernel, shifts, counts),
        out_shape=(
            pltpu.VMEM(own.shape, BF16),
            pltpu.VMEM(own.shape, BF16),
            pltpu.VMEM((2 * rows, features), F32),
        ),
        in_specs=[SMEM, SMEM] + [VMEM] * len(given),
        out_specs=(VMEM,) * 3,
        compiler_params=PARAMS,
        name="update",
    )(x, z_lo, *[near_memory(v) for v in given])


def gradient_kernel(core, mine, theirs, signal_own, signal_other, own, other, out, codes_out, buf, sems, piece_sems):
    width = own.shape[1] // 8
    copies = []
    for q in range(8):
        target = codes_out.at[:, columns(2 * q + core[0], width)]
        copies.append(pltpu.make_async_copy(own.at[:, columns(q, width)], target, sems.at[q]))
    misfit = misfit_of(mine, theirs, signal_own, signal_other)
    wide = jnp.concatenate([misfit, misfit[:, 128:192]], axis=1)
    part = width // 8
    low = lax.broadcasted_iota(jnp.int32, (part // 2, 128), 1) < 64
    for q in range(8):
        span = slice(q * width, (q + 1) * width)
        codes = jnp.concatenate([own[:, span], other[:, span]], axis=0)
        product = lax.dot_general(codes, wide, (((0,), (0,)), ((), ())), preferred_element_type=F32)
        for n in range(8):
            piece = product[n * part : (n + 1) * part]
            buf[q * 8 + n, 0:part] = piece[:, 0:128].astype(BF16)
            tail = jnp.where(low, piece[: part // 2, 128:256], piece[part // 2 :, 128:256])
            buf[q * 8 + n, part : part + part // 2] = tail.astype(BF16)
        copy = pltpu.make_async_copy(buf.at[q * 8 : q * 8 + 8], out.at[q * 8 : q * 8 + 8], piece_sems.at[q])
        copy.start()
        copies.append(copy)
        copies[q].start()
    for copy in copies:
        copy.wait()


def gradient(core, mine, theirs, signal_own, signal_other, own, other):
    part = own.shape[1] // 64
    given = [mine, theirs, signal_own, signal_other, own, other]
    pieces = (64, part + part // 2, 128)
    return pl.pallas_call(
        gradient_kernel,
        out_shape=(
            pltpu.HBM(pieces, BF16),
            pltpu.HBM((own.shape[0], 2 * own.shape[1]), BF16),
        ),
        in_specs=[SMEM] + [VMEM] * 6,
        out_specs=(ANY, ANY),
        scratch_shapes=[
            pltpu.VMEM(pieces, BF16),
            pltpu.SemaphoreType.DMA((8,)),
            pltpu.SemaphoreType.DMA((8,)),
        ],
        compiler_params=PARAMS,
        name="gradient",
    )(core, *[near_memory(v) for v in given])


def place_kernel(core, fresh_back, codes, codes_out, sems):
    width = fresh_back.shape[1] // 8
    copies = []
    for q in range(8):
        target = codes_out.at[:, columns(2 * q + 1 - core[0], width)]
        copies.append(pltpu.make_async_copy(fresh_back.at[:, columns(q, width)], target, sems.at[q]))
    for copy in copies:
        copy.start()
    for copy in copies:
        copy.wait()


def place(core, fresh_back, codes):
    return pl.pallas_call(
        place_kernel,
        out_shape=pltpu.HBM(codes.shape, BF16),
        in_specs=[SMEM, VMEM, ANY],
        out_specs=ANY,
        scratch_shapes=[pltpu.SemaphoreType.DMA((8,))],
        input_output_aliases={2: 0},
        compiler_params=PARAMS,
        name="place",
    )(core, near_memory(fresh_back), far_memory(codes))


def finish_kernel(scale, pieces, grad_out):
    part = grad_out.shape[0]
    total = pieces[0].astype(F32)
    for i in range(1, pieces.shape[0]):
        total = total + pieces[i].astype(F32)
    total = total * scale
    grad_out[:, 0:128] = total[0:part]
    grad_out[0 : part // 2, 128:192] = total[part:, 0:64]
    grad_out[part // 2 :, 128:192] = total[part:, 64:128]


def finish(scale, pieces, grad_shape):
    return pl.pallas_call(
        functools.partial(finish_kernel, scale),
        out_shape=jax.ShapeDtypeStruct(grad_shape, F32),
        in_specs=[VMEM],
        out_specs=VMEM,
        compiler_params=PARAMS,
        name="finish",
    )(near_memory(pieces))


def step(codes, signals, dictionary):
    rows, atom_count = codes.shape
    core, x, z_lo = (lax.axis_index(a).astype(jnp.int32).reshape(1) for a in ("core", "x", "z_lo"))
    atoms = dictionary.T
    mid = atoms.shape[0] // 2
    left = send_x(atoms, 1)
    right = send_x(atoms, -1)
    low, high = halve(core, x, z_lo, atoms)
    near = (send_z(low, 1), send_z(high, -1))
    own, away = split(core, codes)
    other = send_core(away)
    signal_other = send_core(signals)
    far = (send_x(left[:mid], 1), send_x(right[mid:], -1))
    near_left = send_z(left, 1)
    near_right = send_z(right, -1)
    near_far = (send_z(far[0], 1), send_z(far[1], -1))
    plan = [
        ((0, 0), (low, high)),
        ((0, 3), (left,)),
        ((0, 1), (right,)),
        ((1, 0), near),
        ((0, 2), far),
        ((1, 3), (near_left,)),
        ((1, 1), (near_right,)),
        ((1, 2), near_far),
    ]
    shifts = [p[0] for p in plan]
    parts = [p[1] for p in plan]
    mine = None
    for first, last in ((0, 4), (4, 7), (7, 8)):
        mine = estimate(x, z_lo, own, other, mine, shifts[first:last], parts[first:last])
    theirs = send_core(mine)
    fresh_own, fresh_other, second = update(
        x, z_lo, own, other, mine, theirs, signals, signal_other, shifts, parts
    )
    second_theirs = send_core(second)
    fresh_back = send_core(fresh_other)
    pieces, fresh = gradient(core, second, second_theirs, signals, signal_other, fresh_own, fresh_other)
    pieces = functools.partial(lax.all_to_all, tiled=True)(pieces, ("z_lo", "x", "z_hi", "y"), 0, 0)
    fresh = place(core, fresh_back, fresh)
    total_rows = rows
    for size in SIZES:
        total_rows *= size
    grad_shape = (atom_count // 128, signals.shape[1])
    return fresh, finish(float(total_rows) ** -0.5, pieces, grad_shape)


def solution(mesh):
    fine = Mesh(mesh.devices.reshape(SIZES), AXES)
    every = P(AXES, None)
    return jax.shard_map(
        step,
        mesh=fine,
        in_specs=(every, every, P(("z_lo", "x", "core"), None)),
        out_specs=(every, every),
        check_vma=False,
    )
```

profile of v0, /device:TPU:0, one launch (start us, length us, event | category | flops | bytes accessed | tf_op | source)
XLA Modules:
  0.0 91.5 jit_solution(14080628105928201491)
XLA Ops:
  0.6 3.9 %split.1 = (bf16[192,6144]{1,0:T(8,128)(2,1)S(1)}, bf16[192,6144]{1,0:T(8,128)(2,1)}) custom-call(s32[1]{0:T(128)} %bitcast.core, bf16[192,12288]{1,0:T(8,128)(2,1)} %codes.1), custom_call_target="tpu_custom_call" | custom-call | tf_op jit(solution)/shard_map/split/pallas_call | solution.py:103
  4.7 2.9 %collective-permute-start.2 = (bf16[192,768]{1,0:T(8,128)(2,1)S(1)}, bf16[192,768]{1,0:T(8,128)(2,1)S(1)}, u32[]{:S(2)}, u32[]{:S(2)}) collective-permute-start(bf16[192,768]{1,0:T(8,128)(2,1)S(1)} %bitcast.5), channel_id=1, source_target_pairs={{0,48},{16,0},{32,16},{48,32},{1,49},{17,1},{33,17},{49,33},{2,50}... | collective-permute-start | bytes 884744 | tf_op jit(solution)/shard_map/ppermute | solution.py:37
  7.6 1.0 %halve.1 = (bf16[96,768]{1,0:T(8,128)(2,1)S(1)}, bf16[96,768]{1,0:T(8,128)(2,1)S(1)}) custom-call(s32[1]{0:T(128)} %bitcast.core, s32[1]{0:T(128)} %bitcast.1.x, s32[1]{0:T(128)} %bitcast.2.z_lo, bf16[192,768]{1,0:T(8,128)(2,1)} %bitcast.4), custom_call_target="tpu_custom_call" | custom-call | tf_op jit(solution)/shard_map/halve/pallas_call | solution.py:71
  8.6 2.0 %collective-permute-start.3 = (bf16[96,768]{1,0:T(8,128)(2,1)S(1)}, bf16[96,768]{1,0:T(8,128)(2,1)S(1)}, u32[]{:S(2)}, u32[]{:S(2)}) collective-permute-start(bf16[96,768]{1,0:T(8,128)(2,1)S(1)} %get-tuple-element.13.refs_0_), channel_id=1, source_target_pairs={{0,64},{64,4},{4,68},{68,0},{1,65},{65,5},{5,69},{69,1},{2,66},{66... | collective-permute-start | bytes 442376 | tf_op jit(solution)/shard_map/ppermute | solution.py:41
  10.6 2.2 %collective-permute-start.4 = (bf16[96,768]{1,0:T(8,128)(2,1)S(1)}, bf16[96,768]{1,0:T(8,128)(2,1)S(1)}, u32[]{:S(2)}, u32[]{:S(2)}) collective-permute-start(bf16[96,768]{1,0:T(8,128)(2,1)S(1)} %get-tuple-element.14.refs_1_), channel_id=1, source_target_pairs={{0,68},{64,0},{4,64},{68,4},{1,69},{65,1},{5,65},{69,5},{2,70},{66... | collective-permute-start | bytes 442376 | tf_op jit(solution)/shard_map/ppermute | solution.py:41
  12.8 1.7 %collective-permute-done.2.refs_3_ = bf16[192,768]{1,0:T(8,128)(2,1)S(1)} collective-permute-done((bf16[192,768]{1,0:T(8,128)(2,1)S(1)}, bf16[192,768]{1,0:T(8,128)(2,1)S(1)}, u32[]{:S(2)}, u32[]{:S(2)}) %collective-permute-start.2) | collective-permute-done | bytes 294944 | tf_op jit(solution)/shard_map/ppermute | solution.py:37
  14.5 3.8 %collective-permute-start.6 = (bf16[96,768]{1,0:T(8,128)(2,1)S(1)}, bf16[96,768]{1,0:T(8,128)(2,1)S(1)}, u32[]{:S(2)}, u32[]{:S(2)}) collective-permute-start(bf16[96,768]{1,0:T(8,128)(2,1)S(1)} %slice.9), channel_id=1, source_target_pairs={{0,48},{16,0},{32,16},{48,32},{1,49},{17,1},{33,17},{49,33},{2,50}... | collective-permute-start | bytes 442376 | tf_op jit(solution)/shard_map/ppermute | solution.py:37
  18.2 2.0 %collective-permute-start.7 = (bf16[192,768]{1,0:T(8,128)(2,1)S(1)}, bf16[192,768]{1,0:T(8,128)(2,1)S(1)}, u32[]{:S(2)}, u32[]{:S(2)}) collective-permute-start(bf16[192,768]{1,0:T(8,128)(2,1)S(1)} %collective-permute-done.1.refs_2_), channel_id=1, source_target_pairs={{0,64},{64,4},{4,68},{68,0},{1,65},{65,5},{5,69},{69,1},{2,66},{66... | collective-permute-start | bytes 884744 | tf_op jit(solution)/shard_map/ppermute | solution.py:41
  20.2 2.2 %collective-permute-start.8 = (bf16[192,768]{1,0:T(8,128)(2,1)S(1)}, bf16[192,768]{1,0:T(8,128)(2,1)S(1)}, u32[]{:S(2)}, u32[]{:S(2)}) collective-permute-start(bf16[192,768]{1,0:T(8,128)(2,1)S(1)} %collective-permute-done.2.refs_3_), channel_id=1, source_target_pairs={{0,68},{64,0},{4,64},{68,4},{1,69},{65,1},{5,65},{69,5},{2,70},{66... | collective-permute-start | bytes 884744 | tf_op jit(solution)/shard_map/ppermute | solution.py:41
  22.5 2.6 %collective-permute-start.10 = (bf16[96,768]{1,0:T(8,128)(2,1)S(1)}, bf16[96,768]{1,0:T(8,128)(2,1)S(1)}, u32[]{:S(2)}, u32[]{:S(2)}) collective-permute-start(bf16[96,768]{1,0:T(8,128)(2,1)S(1)} %collective-permute-done.6.refs_2_.refs_7_), channel_id=1, source_target_pairs={{0,68},{64,0},{4,64},{68,4},{1,69},{65,1},{5,65},{69,5},{2,70},{66... | collective-permute-start | bytes 442376 | tf_op jit(solution)/shard_map/ppermute | solution.py:41
  25.1 3.7 %collective-permute-done.5.refs_1_.refs_6_ = bf16[96,768]{1,0:T(8,128)(2,1)S(1)} collective-permute-done((bf16[96,768]{1,0:T(8,128)(2,1)S(1)}, bf16[96,768]{1,0:T(8,128)(2,1)S(1)}, u32[]{:S(2)}, u32[]{:S(2)}) %collective-permute-start.5) | collective-permute-done | bytes 147488 | tf_op jit(solution)/shard_map/ppermute | solution.py:37
  28.8 2.5 %estimate.3.refs_0_ = f32[384,192]{1,0:T(8,128)S(1)} custom-call(s32[1]{0:T(128)} %bitcast.1.x, s32[1]{0:T(128)} %bitcast.2.z_lo, bf16[192,6144]{1,0:T(8,128)(2,1)S(1)} %get-tuple-element.11.own, bf16[192,6144]{1,0:T(8,128)(2,1)} %collective-permute-done.other, bf16[96,768]{1,0:T(8,128)(2,1)S(1)} %get-tuple-element.13.refs_0_, ...), custom_call_target="tpu_custom_call" | custom-call | tf_op jit(solution)/shard_map/estimate/pallas_call | solution.py:156
  31.3 2.3 %estimate.4.refs_0_ = f32[384,192]{1,0:T(8,128)S(1)} custom-call(s32[1]{0:T(128)} %bitcast.1.x, s32[1]{0:T(128)} %bitcast.2.z_lo, bf16[192,6144]{1,0:T(8,128)(2,1)S(1)} %get-tuple-element.11.own, bf16[192,6144]{1,0:T(8,128)(2,1)} %collective-permute-done.other, f32[384,192]{1,0:T(8,128)S(1)} %estimate.3.refs_0_, ...), custom_call_target="tpu_custom_call" | custom-call | tf_op jit(solution)/shard_map/estimate/pallas_call | solution.py:156
  33.7 1.5 %collective-permute-done.9.refs_1_.refs_10_ = bf16[96,768]{1,0:T(8,128)(2,1)S(1)} collective-permute-done((bf16[96,768]{1,0:T(8,128)(2,1)S(1)}, bf16[96,768]{1,0:T(8,128)(2,1)S(1)}, u32[]{:S(2)}, u32[]{:S(2)}) %collective-permute-start.9) | collective-permute-done | bytes 147488 | tf_op jit(solution)/shard_map/ppermute | solution.py:41
  35.2 2.0 %estimate.5.mine = f32[384,192]{1,0:T(8,128)S(1)} custom-call(s32[1]{0:T(128)} %bitcast.1.x, s32[1]{0:T(128)} %bitcast.2.z_lo, bf16[192,6144]{1,0:T(8,128)(2,1)S(1)} %get-tuple-element.11.own, bf16[192,6144]{1,0:T(8,128)(2,1)} %collective-permute-done.other, f32[384,192]{1,0:T(8,128)S(1)} %estimate.4.refs_0_, ...), custom_call_target="tpu_custom_call" | custom-call | tf_op jit(solution)/shard_map/estimate/pallas_call | solution.py:156
  37.3 0.5 collective-permute-start.12
  37.8 1.4 %collective-permute-done.12.signal_other = bf16[192,192]{1,0:T(8,128)(2,1)S(1)} collective-permute-done((bf16[192,192]{1,0:T(8,128)(2,1)S(1)}, bf16[192,192]{1,0:T(8,128)(2,1)S(1)}, u32[]{:S(2)}, u32[]{:S(2)}) %collective-permute-start.12) | collective-permute-done | bytes 73760 | tf_op jit(solution)/shard_map/ppermute | solution.py:45
  39.1 5.8 %update.1 = (bf16[192,6144]{1,0:T(8,128)(2,1)S(1)}, bf16[192,6144]{1,0:T(8,128)(2,1)}, f32[384,192]{1,0:T(8,128)S(1)}) custom-call(s32[1]{0:T(128)} %bitcast.1.x, s32[1]{0:T(128)} %bitcast.2.z_lo, bf16[192,6144]{1,0:T(8,128)(2,1)S(1)} %get-tuple-element.11.own, bf16[192,6144]{1,0:T(8,128)(2,1)} %collective-permute-done.other, f32[384,192]{1,0:T(8,128)S(1)} %estimate.5.mine, ...), custom_call_target="tpu_custom_call" | custom-call | tf_op jit(solution)/shard_map/update/pallas_call | solution.py:200
  45.5 1.2 %collective-permute-done.14.theirs = f32[384,192]{1,0:T(8,128)S(1)} collective-permute-done((f32[384,192]{1,0:T(8,128)S(1)}, f32[384,192]{1,0:T(8,128)S(1)}, u32[]{:S(2)}, u32[]{:S(2)}) %collective-permute-start.14) | collective-permute-done | bytes 294944 | tf_op jit(solution)/shard_map/ppermute | solution.py:45
  46.7 5.2 %gradient.1 = (bf16[64,144,128]{2,1,0:T(8,128)(2,1)}, bf16[192,12288]{1,0:T(8,128)(2,1)}) custom-call(s32[1]{0:T(128)} %bitcast.core, f32[384,192]{1,0:T(8,128)S(1)} %get-tuple-element.16.mine, f32[384,192]{1,0:T(8,128)S(1)} %collective-permute-done.14.theirs, bf16[192,192]{1,0:T(8,128)(2,1)S(1)} %copy-done, ...), custom_call_target="tpu_custom_call" | custom-call | tf_op jit(solution)/shard_map/gradient/pallas_call | solution.py:245
  51.9 6.9 %all-to-all-start = ((bf16[64,144,128]{2,1,0:T(8,128)(2,1)}), bf16[64,144,128]{2,1,0:T(8,128)(2,1)S(1)}, u32[]{:S(2)}, u32[]{:S(2)}) async-start(bf16[64,144,128]{2,1,0:T(8,128)(2,1)} %get-tuple-element.19), calls=%async_computation | async-start | bytes 4718592 | tf_op jit(solution)/shard_map/all_to_all | solution.py:348
  58.8 3.1 %place.1 = bf16[192,12288]{1,0:T(8,128)(2,1)} custom-call(s32[1]{0:T(128)} %bitcast.core, bf16[192,6144]{1,0:T(8,128)(2,1)} %collective-permute-done.13.fresh_back, bf16[192,12288]{1,0:T(8,128)(2,1)} %get-tuple-element.18.codes), custom_call_target="tpu_custom_call", output_to_operand_aliasing={{}: (2, {})} | custom-call | tf_op jit(solution)/shard_map/place/pallas_call | solution.py:276
  61.9 28.6 %all-to-all-done.pieces = bf16[64,144,128]{2,1,0:T(8,128)(2,1)S(1)} async-done(((bf16[64,144,128]{2,1,0:T(8,128)(2,1)}), bf16[64,144,128]{2,1,0:T(8,128)(2,1)S(1)}, u32[]{:S(2)}, u32[]{:S(2)}) %all-to-all-start) | async-done | bytes 2359328 | tf_op jit(solution)/shard_map/all_to_all | solution.py:348
  90.5 1.0 %finish.1 = f32[96,192]{1,0:T(8,128)} custom-call(bf16[64,144,128]{2,1,0:T(8,128)(2,1)S(1)} %all-to-all-done.pieces), custom_call_target="tpu_custom_call" | custom-call | tf_op jit(solution)/shard_map/finish/pallas_call | solution.py:300
  (23 shorter events, 0.8 us)
Async XLA Ops:
  0.6 4.0 %copy-start.1 = (bf16[768,192]{0,1:T(8,128)(2,1)S(1)}, bf16[768,192]{0,1:T(8,128)(2,1)}, u32[]{:S(2)}) copy-start(bf16[768,192]{0,1:T(8,128)(2,1)} %param.5) | copy-start | bytes 884740
  4.6 24.3 %collective-permute-start = (bf16[192,6144]{1,0:T(8,128)(2,1)}, bf16[192,6144]{1,0:T(8,128)(2,1)}, u32[]{:S(2)}, u32[]{:S(2)}) collective-permute-start(bf16[192,6144]{1,0:T(8,128)(2,1)} %get-tuple-element.12), channel_id=1, source_target_pairs={{0,8},{8,0},{1,9},{9,1},{2,10},{10,2},{3,11},{11,3},{4,12},{12,4},... | collective-permute-start | bytes 7077896 | tf_op jit(solution)/shard_map/ppermute | solution.py:45
  4.7 9.8 %collective-permute-start.2 = (bf16[192,768]{1,0:T(8,128)(2,1)S(1)}, bf16[192,768]{1,0:T(8,128)(2,1)S(1)}, u32[]{:S(2)}, u32[]{:S(2)}) collective-permute-start(bf16[192,768]{1,0:T(8,128)(2,1)S(1)} %bitcast.5), channel_id=1, source_target_pairs={{0,48},{16,0},{32,16},{48,32},{1,49},{17,1},{33,17},{49,33},{2,50}... | collective-permute-start | bytes 884744 | tf_op jit(solution)/shard_map/ppermute | solution.py:37
  7.6 10.6 %collective-permute-start.1 = (bf16[192,768]{1,0:T(8,128)(2,1)S(1)}, bf16[192,768]{1,0:T(8,128)(2,1)S(1)}, u32[]{:S(2)}, u32[]{:S(2)}) collective-permute-start(bf16[192,768]{1,0:T(8,128)(2,1)S(1)} %bitcast.6), channel_id=1, source_target_pairs={{0,16},{16,32},{32,48},{48,0},{1,17},{17,33},{33,49},{49,1},{2,18}... | collective-permute-start | bytes 884744 | tf_op jit(solution)/shard_map/ppermute | solution.py:37
  8.6 11.6 %collective-permute-start.3 = (bf16[96,768]{1,0:T(8,128)(2,1)S(1)}, bf16[96,768]{1,0:T(8,128)(2,1)S(1)}, u32[]{:S(2)}, u32[]{:S(2)}) collective-permute-start(bf16[96,768]{1,0:T(8,128)(2,1)S(1)} %get-tuple-element.13.refs_0_), channel_id=1, source_target_pairs={{0,64},{64,4},{4,68},{68,0},{1,65},{65,5},{5,69},{69,1},{2,66},{66... | collective-permute-start | bytes 442376 | tf_op jit(solution)/shard_map/ppermute | solution.py:41
  10.6 11.9 %collective-permute-start.4 = (bf16[96,768]{1,0:T(8,128)(2,1)S(1)}, bf16[96,768]{1,0:T(8,128)(2,1)S(1)}, u32[]{:S(2)}, u32[]{:S(2)}) collective-permute-start(bf16[96,768]{1,0:T(8,128)(2,1)S(1)} %get-tuple-element.14.refs_1_), channel_id=1, source_target_pairs={{0,68},{64,0},{4,64},{68,4},{1,69},{65,1},{5,65},{69,5},{2,70},{66... | collective-permute-start | bytes 442376 | tf_op jit(solution)/shard_map/ppermute | solution.py:41
  14.5 8.0 %collective-permute-start.6 = (bf16[96,768]{1,0:T(8,128)(2,1)S(1)}, bf16[96,768]{1,0:T(8,128)(2,1)S(1)}, u32[]{:S(2)}, u32[]{:S(2)}) collective-permute-start(bf16[96,768]{1,0:T(8,128)(2,1)S(1)} %slice.9), channel_id=1, source_target_pairs={{0,48},{16,0},{32,16},{48,32},{1,49},{17,1},{33,17},{49,33},{2,50}... | collective-permute-start | bytes 442376 | tf_op jit(solution)/shard_map/ppermute | solution.py:37
  18.2 13.0 %collective-permute-start.7 = (bf16[192,768]{1,0:T(8,128)(2,1)S(1)}, bf16[192,768]{1,0:T(8,128)(2,1)S(1)}, u32[]{:S(2)}, u32[]{:S(2)}) collective-permute-start(bf16[192,768]{1,0:T(8,128)(2,1)S(1)} %collective-permute-done.1.refs_2_), channel_id=1, source_target_pairs={{0,64},{64,4},{4,68},{68,0},{1,65},{65,5},{5,69},{69,1},{2,66},{66... | collective-permute-start | bytes 884744 | tf_op jit(solution)/shard_map/ppermute | solution.py:41
  20.2 11.1 %collective-permute-start.8 = (bf16[192,768]{1,0:T(8,128)(2,1)S(1)}, bf16[192,768]{1,0:T(8,128)(2,1)S(1)}, u32[]{:S(2)}, u32[]{:S(2)}) collective-permute-start(bf16[192,768]{1,0:T(8,128)(2,1)S(1)} %collective-permute-done.2.refs_3_), channel_id=1, source_target_pairs={{0,68},{64,0},{4,64},{68,4},{1,69},{65,1},{5,65},{69,5},{2,70},{66... | collective-permute-start | bytes 884744 | tf_op jit(solution)/shard_map/ppermute | solution.py:41
  22.5 6.4 %collective-permute-start.5 = (bf16[96,768]{1,0:T(8,128)(2,1)S(1)}, bf16[96,768]{1,0:T(8,128)(2,1)S(1)}, u32[]{:S(2)}, u32[]{:S(2)}) collective-permute-start(bf16[96,768]{1,0:T(8,128)(2,1)S(1)} %slice.8), channel_id=1, source_target_pairs={{0,16},{16,32},{32,48},{48,0},{1,17},{17,33},{33,49},{49,1},{2,18}... | collective-permute-start | bytes 442376 | tf_op jit(solution)/shard_map/ppermute | solution.py:37
  22.5 11.2 %collective-permute-start.10 = (bf16[96,768]{1,0:T(8,128)(2,1)S(1)}, bf16[96,768]{1,0:T(8,128)(2,1)S(1)}, u32[]{:S(2)}, u32[]{:S(2)}) collective-permute-start(bf16[96,768]{1,0:T(8,128)(2,1)S(1)} %collective-permute-done.6.refs_2_.refs_7_), channel_id=1, source_target_pairs={{0,68},{64,0},{4,64},{68,4},{1,69},{65,1},{5,65},{69,5},{2,70},{66... | collective-permute-start | bytes 442376 | tf_op jit(solution)/shard_map/ppermute | solution.py:41
  28.8 6.4 %collective-permute-start.9 = (bf16[96,768]{1,0:T(8,128)(2,1)S(1)}, bf16[96,768]{1,0:T(8,128)(2,1)S(1)}, u32[]{:S(2)}, u32[]{:S(2)}) collective-permute-start(bf16[96,768]{1,0:T(8,128)(2,1)S(1)} %collective-permute-done.5.refs_1_.refs_6_), channel_id=1, source_target_pairs={{0,64},{64,4},{4,68},{68,0},{1,65},{65,5},{5,69},{69,1},{2,66},{66... | collective-permute-start | bytes 442376 | tf_op jit(solution)/shard_map/ppermute | solution.py:41
  33.6 3.6 %copy-start = (bf16[192,192]{1,0:T(8,128)(2,1)S(1)}, bf16[192,192]{1,0:T(8,128)(2,1)}, u32[]{:S(2)}) copy-start(bf16[192,192]{1,0:T(8,128)(2,1)} %signal_own.3) | copy-start | bytes 221188
  37.2 1.9 %collective-permute-start.11 = (f32[384,192]{1,0:T(8,128)S(1)}, f32[384,192]{1,0:T(8,128)S(1)}, u32[]{:S(2)}, u32[]{:S(2)}) collective-permute-start(f32[384,192]{1,0:T(8,128)S(1)} %estimate.5.mine), channel_id=1, source_target_pairs={{0,8},{8,0},{1,9},{9,1},{2,10},{10,2},{3,11},{11,3},{4,12},{12,4},... | collective-permute-start | bytes 884744 | tf_op jit(solution)/shard_map/ppermute | solution.py:45
  37.3 1.8 %collective-permute-start.12 = (bf16[192,192]{1,0:T(8,128)(2,1)S(1)}, bf16[192,192]{1,0:T(8,128)(2,1)S(1)}, u32[]{:S(2)}, u32[]{:S(2)}) collective-permute-start(bf16[192,192]{1,0:T(8,128)(2,1)S(1)} %copy-done), channel_id=1, source_target_pairs={{0,8},{8,0},{1,9},{9,1},{2,10},{10,2},{3,11},{11,3},{4,12},{12,4},... | collective-permute-start | bytes 221192 | tf_op jit(solution)/shard_map/ppermute | solution.py:45
  44.9 1.7 %collective-permute-start.14 = (f32[384,192]{1,0:T(8,128)S(1)}, f32[384,192]{1,0:T(8,128)S(1)}, u32[]{:S(2)}, u32[]{:S(2)}) collective-permute-start(f32[384,192]{1,0:T(8,128)S(1)} %get-tuple-element.16.mine), channel_id=1, source_target_pairs={{0,8},{8,0},{1,9},{9,1},{2,10},{10,2},{3,11},{11,3},{4,12},{12,4},... | collective-permute-start | bytes 884744 | tf_op jit(solution)/shard_map/ppermute | solution.py:45
  45.1 13.7 %collective-permute-start.13 = (bf16[192,6144]{1,0:T(8,128)(2,1)}, bf16[192,6144]{1,0:T(8,128)(2,1)}, u32[]{:S(2)}, u32[]{:S(2)}) collective-permute-start(bf16[192,6144]{1,0:T(8,128)(2,1)} %get-tuple-element.15.other), channel_id=1, source_target_pairs={{0,8},{8,0},{1,9},{9,1},{2,10},{10,2},{3,11},{11,3},{4,12},{12,4},... | collective-permute-start | bytes 7077896 | tf_op jit(solution)/shard_map/ppermute | solution.py:45
  51.9 38.7 %all-to-all-start = ((bf16[64,144,128]{2,1,0:T(8,128)(2,1)}), bf16[64,144,128]{2,1,0:T(8,128)(2,1)S(1)}, u32[]{:S(2)}, u32[]{:S(2)}) async-start(bf16[64,144,128]{2,1,0:T(8,128)(2,1)} %get-tuple-element.19), calls=%async_computation | async-start | bytes 4718592 | tf_op jit(solution)/shard_map/all_to_all | solution.py:348
where the time goes:
time: 93.1 us; the launch traced here: 91.5 us
  waiting for transfers between devices  38.1 us (41%)
  Pallas kernels  26.8 us (29%)
  starting transfers between devices  25.8 us (28%)
    all_to_all x1, waiting for transfers between devices, step(): functools.partial(lax.all_to_all, tiled=True)  28.6 us
    ppermute x6, starting transfers between devices, send_z(): return lax.ppermute(value, ('z_lo', 'z_hi'), z_step(step))  11 us
    all_to_all x1, starting transfers between devices, step(): functools.partial(lax.all_to_all, tiled=True)  6.88 us
    pallas_call x3, Pallas kernels, estimate(): pl.pallas_call(functools.partial(estimate_kernel, shifts, counts, start i...  6.8 us
    ppermute x4, starting transfers between devices, send_x(): return lax.ppermute(value, 'x', [(i, (i + step) % 4) for i in range(4)])  6.71 us
    pallas_call x1, Pallas kernels, update(): pl.pallas_call(functools.partial(update_kernel, shifts, counts), out_shap...  5.83 us
    ppermute x4, waiting for transfers between devices, send_x(): return lax.ppermute(value, 'x', [(i, (i + step) % 4) for i in range(4)])  5.36 us
    pallas_call x1, Pallas kernels, gradient(): pl.pallas_call(gradient_kernel, out_shape=(pltpu.HBM(pieces, BF16), pltpu...  5.18 us
  transfers between devices with their start and end apart: 16, of which 6 were waited for; matrix products, arithmetic and copies ran while one was open for 0% of the time, Pallas kernels for 15%

commit v1 on v0

--- a/solution.py
+++ b/solution.py
@@ -79,35 +79,28 @@
     )(core, x, z_lo, far_memory(atoms))
 
 
-def split_kernel(core, codes, own, away, sems):
-    width = own.shape[1] // 8
+def take_kernel(core, codes, out, sems):
+    width = out.shape[1] // 8
     copies = []
-    for side, (target, half) in enumerate(((away, 1 - core[0]), (own, core[0]))):
-        for q in range(8):
-            copies.append(
-                pltpu.make_async_copy(
-                    codes.at[:, columns(2 * q + half, width)],
-                    target.at[:, columns(q, width)],
-                    sems.at[side, q],
-                )
-            )
+    for q in range(8):
+        source = codes.at[:, columns(2 * q + core[0], width)]
+        copies.append(pltpu.make_async_copy(source, out.at[:, columns(q, width)], sems.at[q]))
     for copy in copies:
         copy.start()
     for copy in copies:
         copy.wait()
 
 
-def split(core, codes):
+def take_half(core, codes):
     rows, atom_count = codes.shape
-    half = pltpu.VMEM((rows, atom_count // 2), BF16)
-    return pl.pallas_call(
-        split_kernel,
-        out_shape=(half, half),
+    return pl.pallas_call(
+        take_kernel,
+        out_shape=pltpu.VMEM((rows, atom_count // 2), BF16),
         in_specs=[SMEM, ANY],
-        out_specs=(VMEM, VMEM),
-        scratch_shapes=[pltpu.SemaphoreType.DMA((2, 8))],
-        compiler_params=PARAMS,
-        name="split",
+        out_specs=VMEM,
+        scratch_shapes=[pltpu.SemaphoreType.DMA((8,))],
+        compiler_params=PARAMS,
+        name="take",
     )(core, far_memory(codes))
 
 
@@ -170,9 +163,10 @@
     return jnp.concatenate([first.astype(BF16), second.astype(BF16)], axis=0)
 
 
-def update_kernel(shifts, counts, x, z_lo, own, other, mine, theirs, signal_own, signal_other, *refs):
+def update_kernel(shifts, counts, core, x, z_lo, own, other, mine, theirs, signal_own, signal_other, *refs):
     parts, rest = take(refs, counts)
-    fresh_own, fresh_other, out = rest
+    fresh_own, fresh_other, out, codes_out, back, sems = rest
+    copies = []
     rows = own.shape[0]
     width = own.shape[1] // 8
     misfit = misfit_of(mine, theirs, signal_own, signal_other)
@@ -184,14 +178,23 @@
             value = source[:, span].astype(F32) - 4.0 * correlation
             fresh = (value - jnp.clip(value, -0.5, 0.5)).astype(BF16)
             target[:, span] = fresh
+            if target is fresh_own:
+                block = 2 * chunk_place(shifts[k], x, z_lo) + core[0]
+                copy = pltpu.make_async_copy(target.at[:, span], codes_out.at[:, columns(block, width)], sems.at[0, k])
+            else:
+                copy = pltpu.make_async_copy(target.at[:, span], back.at[:, span], sems.at[1, k])
+            copy.start()
+            copies.append(copy)
             term = along_atoms(fresh, atoms)
             if k:
                 out[low : low + rows] += term
             else:
                 out[low : low + rows] = term
-
-
-def update(x, z_lo, own, other, mine, theirs, signal_own, signal_other, shifts, parts):
+    for copy in copies:
+        copy.wait()
+
+
+def update(core, x, z_lo, own, other, mine, theirs, signal_own, signal_other, shifts, parts):
     rows = own.shape[0]
     features = sum(p.shape[0] for p in parts[0])
     counts = tuple(len(p) for p in parts)
@@ -203,20 +206,20 @@
             pltpu.VMEM(own.shape, BF16),
             pltpu.VMEM(own.shape, BF16),
             pltpu.VMEM((2 * rows, features), F32),
+            pltpu.HBM((rows, 2 * own.shape[1]), BF16),
+            pltpu.HBM(own.shape, BF16),
         ),
-        in_specs=[SMEM, SMEM] + [VMEM] * len(given),
-        out_specs=(VMEM,) * 3,
+        in_specs=[SMEM] * 3 + [VMEM] * len(given),
+        out_specs=(VMEM,) * 3 + (ANY, ANY),
+        scratch_shapes=[pltpu.SemaphoreType.DMA((2, len(parts)))],
         compiler_params=PARAMS,
         name="update",
-    )(x, z_lo, *[near_memory(v) for v in given])
-
-
-def gradient_kernel(core, mine, theirs, signal_own, signal_other, own, other, out, codes_out, buf, sems, piece_sems):
+    )(core, x, z_lo, *[near_memory(v) for v in given])
+
+
+def gradient_kernel(mine, theirs, signal_own, signal_other, own, other, out, buf, sems):
     width = own.shape[1] // 8
     copies = []
-    for q in range(8):
-        target = codes_out.at[:, columns(2 * q + core[0], width)]
-        copies.append(pltpu.make_async_copy(own.at[:, columns(q, width)], target, sems.at[q]))
     misfit = misfit_of(mine, theirs, signal_own, signal_other)
     wide = jnp.concatenate([misfit, misfit[:, 128:192]], axis=1)
     part = width // 8
@@ -230,34 +233,26 @@
             buf[q * 8 + n, 0:part] = piece[:, 0:128].astype(BF16)
             tail = jnp.where(low, piece[: part // 2, 128:256], piece[part // 2 :, 128:256])
             buf[q * 8 + n, part : part + part // 2] = tail.astype(BF16)
-        copy = pltpu.make_async_copy(buf.at[q * 8 : q * 8 + 8], out.at[q * 8 : q * 8 + 8], piece_sems.at[q])
+        copy = pltpu.make_async_copy(buf.at[q * 8 : q * 8 + 8], out.at[q * 8 : q * 8 + 8], sems.at[q])
         copy.start()
         copies.append(copy)
-        copies[q].start()
-    for copy in copies:
-        copy.wait()
-
-
-def gradient(core, mine, theirs, signal_own, signal_other, own, other):
+    for copy in copies:
+        copy.wait()
+
+
+def gradient(mine, theirs, signal_own, signal_other, own, other):
     part = own.shape[1] // 64
     given = [mine, theirs, signal_own, signal_other, own, other]
     pieces = (64, part + part // 2, 128)
     return pl.pallas_call(
         gradient_kernel,
-        out_shape=(
-            pltpu.HBM(pieces, BF16),
-            pltpu.HBM((own.shape[0], 2 * own.shape[1]), BF16),
-        ),
-        in_specs=[SMEM] + [VMEM] * 6,
-        out_specs=(ANY, ANY),
-        scratch_shapes=[
-            pltpu.VMEM(pieces, BF16),
-            pltpu.SemaphoreType.DMA((8,)),
-            pltpu.SemaphoreType.DMA((8,)),
-        ],
+        out_shape=pltpu.HBM(pieces, BF16),
+        in_specs=[VMEM] * 6,
+        out_specs=ANY,
+        scratch_shapes=[pltpu.VMEM(pieces, BF16), pltpu.SemaphoreType.DMA((8,))],
         compiler_params=PARAMS,
         name="gradient",
-    )(core, *[near_memory(v) for v in given])
+    )(*[near_memory(v) for v in given])
 
 
 def place_kernel(core, fresh_back, codes, codes_out, sems):
@@ -316,8 +311,9 @@
     right = send_x(atoms, -1)
     low, high = halve(core, x, z_lo, atoms)
     near = (send_z(low, 1), send_z(high, -1))
-    own, away = split(core, codes)
+    away = take_half(1 - core, codes)
     other = send_core(away)
+    own = take_half(core, codes)
     signal_other = send_core(signals)
     far = (send_x(left[:mid], 1), send_x(right[mid:], -1))
     near_left = send_z(left, 1)
@@ -339,12 +335,12 @@
     for first, last in ((0, 4), (4, 7), (7, 8)):
         mine = estimate(x, z_lo, own, other, mine, shifts[first:last], parts[first:last])
     theirs = send_core(mine)
-    fresh_own, fresh_other, second = update(
-        x, z_lo, own, other, mine, theirs, signals, signal_other, shifts, parts
+    fresh_own, fresh_other, second, fresh, back = update(
+        core, x, z_lo, own, other, mine, theirs, signals, signal_other, shifts, parts
     )
     second_theirs = send_core(second)
-    fresh_back = send_core(fresh_other)
-    pieces, fresh = gradient(core, second, second_theirs, signals, signal_other, fresh_own, fresh_other)
+    fresh_back = send_core(back)
+    pieces = gradient(second, second_theirs, signals, signal_other, fresh_own, fresh_other)
     pieces = functools.partial(lax.all_to_all, tiled=True)(pieces, ("z_lo", "x", "z_hi", "y"), 0, 0)
     fresh = place(core, fresh_back, fresh)
     total_rows = rows

time: 93.1 us -> 86.3 us (0.927)
  Pallas kernels: 26.8 us -> 18.4 us
  waiting for transfers between devices: 38.1 us -> 39.2 us
    pallas_call x3, Pallas kernels: 6.8 us -> 1.82 us  [estimate(): pl.pallas_call(functools.partial(estimate_kernel, shifts, counts, start i...]
    pallas_call x1, Pallas kernels: 5.83 us -> 3.71 us  [update(): pl.pallas_call(functools.partial(update_kernel, shifts, counts), out_shap...]
    ppermute x6, waiting for transfers between devices: 1.5 us -> 3.16 us  [send_z(): return lax.ppermute(value, ('z_lo', 'z_hi'), z_step(step))]
    pallas_call x2 -> x3, Pallas kernels: 9.09 us -> 7.72 us  [the longest x2 4.78 us: take_half(): pl.pallas_call(take_kernel, out_shape=pltpu.VMEM((rows, atom_count // 2),...]
  transfers between devices with their start and end apart: 16 -> 16, of which waited for: 6 -> 7; matrix products, arithmetic and copies ran while one was open for 0% -> 0% of each run, Pallas kernels for 15% -> 12%
where the time goes in v1:
time: 86.3 us; the launch traced here: 84.8 us
  waiting for transfers between devices  39.2 us (45%)
  starting transfers between devices  26.4 us (31%)
  Pallas kernels  18.4 us (21%)
    all_to_all x1, waiting for transfers between devices, step(): functools.partial(lax.all_to_all, tiled=True)  28.6 us
    ppermute x6, starting transfers between devices, send_z(): return lax.ppermute(value, ('z_lo', 'z_hi'), z_step(step))  11.5 us
    all_to_all x1, starting transfers between devices, step(): functools.partial(lax.all_to_all, tiled=True)  6.85 us
    ppermute x4, starting transfers between devices, send_x(): return lax.ppermute(value, 'x', [(i, (i + step) % 4) for i in range(4)])  6.78 us
    ppermute x4, waiting for transfers between devices, send_x(): return lax.ppermute(value, 'x', [(i, (i + step) % 4) for i in range(4)])  4.79 us
    pallas_call x2, Pallas kernels, take_half(): pl.pallas_call(take_kernel, out_shape=pltpu.VMEM((rows, atom_count // 2),...  4.78 us
    pallas_call x1, Pallas kernels, update(): pl.pallas_call(functools.partial(update_kernel, shifts, counts), out_shap...  3.71 us
    ppermute x6, waiting for transfers between devices, send_z(): return lax.ppermute(value, ('z_lo', 'z_hi'), z_step(step))  3.16 us
  transfers between devices with their start and end apart: 16, of which 7 were waited for; matrix products, arithmetic and copies ran while one was open for 0% of the time, Pallas kernels for 12%

profile of v1, /device:TPU:0, one launch (start us, length us, event | category | flops | bytes accessed | tf_op | source)
XLA Modules:
  0.0 84.8 jit_solution(14924092189718262242)
XLA Ops:
  0.6 3.1 %take.3 = bf16[192,6144]{1,0:T(8,128)(2,1)} custom-call(s32[1]{0:T(128)S(6)} %sub.3.core, bf16[192,12288]{1,0:T(8,128)(2,1)} %codes.3), custom_call_target="tpu_custom_call" | custom-call | tf_op jit(solution)/shard_map/take/pallas_call | solution.py:96
  3.9 2.9 %collective-permute-start.2 = (bf16[192,768]{1,0:T(8,128)(2,1)S(1)}, bf16[192,768]{1,0:T(8,128)(2,1)S(1)}, u32[]{:S(2)}, u32[]{:S(2)}) collective-permute-start(bf16[192,768]{1,0:T(8,128)(2,1)S(1)} %bitcast.5), channel_id=1, source_target_pairs={{0,48},{16,0},{32,16},{48,32},{1,49},{17,1},{33,17},{49,33},{2,50}... | collective-permute-start | bytes 884744 | tf_op jit(solution)/shard_map/ppermute | solution.py:37
  6.8 1.0 %halve.1 = (bf16[96,768]{1,0:T(8,128)(2,1)S(1)}, bf16[96,768]{1,0:T(8,128)(2,1)S(1)}) custom-call(s32[1]{0:T(128)} %bitcast.core, s32[1]{0:T(128)} %bitcast.1.x, s32[1]{0:T(128)} %bitcast.2.z_lo, bf16[192,768]{1,0:T(8,128)(2,1)} %bitcast.4), custom_call_target="tpu_custom_call" | custom-call | tf_op jit(solution)/shard_map/halve/pallas_call | solution.py:71
  7.8 2.0 %collective-permute-start.3 = (bf16[96,768]{1,0:T(8,128)(2,1)S(1)}, bf16[96,768]{1,0:T(8,128)(2,1)S(1)}, u32[]{:S(2)}, u32[]{:S(2)}) collective-permute-start(bf16[96,768]{1,0:T(8,128)(2,1)S(1)} %get-tuple-element.9.refs_0_), channel_id=1, source_target_pairs={{0,64},{64,4},{4,68},{68,0},{1,65},{65,5},{5,69},{69,1},{2,66},{66... | collective-permute-start | bytes 442376 | tf_op jit(solution)/shard_map/ppermute | solution.py:41
  9.8 2.2 %collective-permute-start.4 = (bf16[96,768]{1,0:T(8,128)(2,1)S(1)}, bf16[96,768]{1,0:T(8,128)(2,1)S(1)}, u32[]{:S(2)}, u32[]{:S(2)}) collective-permute-start(bf16[96,768]{1,0:T(8,128)(2,1)S(1)} %get-tuple-element.10.refs_1_), channel_id=1, source_target_pairs={{0,68},{64,0},{4,64},{68,4},{1,69},{65,1},{5,65},{69,5},{2,70},{66... | collective-permute-start | bytes 442376 | tf_op jit(solution)/shard_map/ppermute | solution.py:41
  12.0 1.7 %collective-permute-done.2.refs_3_ = bf16[192,768]{1,0:T(8,128)(2,1)S(1)} collective-permute-done((bf16[192,768]{1,0:T(8,128)(2,1)S(1)}, bf16[192,768]{1,0:T(8,128)(2,1)S(1)}, u32[]{:S(2)}, u32[]{:S(2)}) %collective-permute-start.2) | collective-permute-done | bytes 294944 | tf_op jit(solution)/shard_map/ppermute | solution.py:37
  13.7 3.8 %collective-permute-start.6 = (bf16[96,768]{1,0:T(8,128)(2,1)S(1)}, bf16[96,768]{1,0:T(8,128)(2,1)S(1)}, u32[]{:S(2)}, u32[]{:S(2)}) collective-permute-start(bf16[96,768]{1,0:T(8,128)(2,1)S(1)} %slice.9), channel_id=1, source_target_pairs={{0,48},{16,0},{32,16},{48,32},{1,49},{17,1},{33,17},{49,33},{2,50}... | collective-permute-start | bytes 442376 | tf_op jit(solution)/shard_map/ppermute | solution.py:37
  17.4 4.0 %collective-permute-start.8 = (bf16[192,768]{1,0:T(8,128)(2,1)S(1)}, bf16[192,768]{1,0:T(8,128)(2,1)S(1)}, u32[]{:S(2)}, u32[]{:S(2)}) collective-permute-start(bf16[192,768]{1,0:T(8,128)(2,1)S(1)} %collective-permute-done.2.refs_3_), channel_id=1, source_target_pairs={{0,68},{64,0},{4,64},{68,4},{1,69},{65,1},{5,65},{69,5},{2,70},{66... | collective-permute-start | bytes 884744 | tf_op jit(solution)/shard_map/ppermute | solution.py:41
  21.7 3.2 %collective-permute-start.10 = (bf16[96,768]{1,0:T(8,128)(2,1)S(1)}, bf16[96,768]{1,0:T(8,128)(2,1)S(1)}, u32[]{:S(2)}, u32[]{:S(2)}) collective-permute-start(bf16[96,768]{1,0:T(8,128)(2,1)S(1)} %collective-permute-done.6.refs_2_.refs_7_), channel_id=1, source_target_pairs={{0,68},{64,0},{4,64},{68,4},{1,69},{65,1},{5,65},{69,5},{2,70},{66... | collective-permute-start | bytes 442376 | tf_op jit(solution)/shard_map/ppermute | solution.py:41
  24.9 3.1 %collective-permute-done.5.refs_1_.refs_6_ = bf16[96,768]{1,0:T(8,128)(2,1)S(1)} collective-permute-done((bf16[96,768]{1,0:T(8,128)(2,1)S(1)}, bf16[96,768]{1,0:T(8,128)(2,1)S(1)}, u32[]{:S(2)}, u32[]{:S(2)}) %collective-permute-start.5) | collective-permute-done | bytes 147488 | tf_op jit(solution)/shard_map/ppermute | solution.py:37
  28.0 1.7 %take.2.own = bf16[192,6144]{1,0:T(8,128)(2,1)S(1)} custom-call(s32[1]{0:T(128)} %bitcast.core, bf16[192,12288]{1,0:T(8,128)(2,1)} %codes.3), custom_call_target="tpu_custom_call" | custom-call | tf_op jit(solution)/shard_map/take/pallas_call | solution.py:96
  29.7 0.8 estimate.3.refs_0_
  30.5 1.0 %collective-permute-done.7.refs_3_.refs_8_ = bf16[192,768]{1,0:T(8,128)(2,1)S(1)} collective-permute-done((bf16[192,768]{1,0:T(8,128)(2,1)S(1)}, bf16[192,768]{1,0:T(8,128)(2,1)S(1)}, u32[]{:S(2)}, u32[]{:S(2)}) %collective-permute-start.7) | collective-permute-done | bytes 294944 | tf_op jit(solution)/shard_map/ppermute | solution.py:41
  31.5 0.7 estimate.4.refs_0_
  32.2 2.2 %collective-permute-done.9.refs_1_.refs_10_ = bf16[96,768]{1,0:T(8,128)(2,1)S(1)} collective-permute-done((bf16[96,768]{1,0:T(8,128)(2,1)S(1)}, bf16[96,768]{1,0:T(8,128)(2,1)S(1)}, u32[]{:S(2)}, u32[]{:S(2)}) %collective-permute-start.9) | collective-permute-done | bytes 147488 | tf_op jit(solution)/shard_map/ppermute | solution.py:41
  34.8 0.5 collective-permute-start.12
  35.3 1.4 %collective-permute-done.12.signal_other = bf16[192,192]{1,0:T(8,128)(2,1)S(1)} collective-permute-done((bf16[192,192]{1,0:T(8,128)(2,1)S(1)}, bf16[192,192]{1,0:T(8,128)(2,1)S(1)}, u32[]{:S(2)}, u32[]{:S(2)}) %collective-permute-start.12) | collective-permute-done | bytes 73760 | tf_op jit(solution)/shard_map/ppermute | solution.py:45
  36.7 3.7 %update.1 = (bf16[192,6144]{1,0:T(8,128)(2,1)S(1)}, bf16[192,6144]{1,0:T(8,128)(2,1)S(1)}, f32[384,192]{1,0:T(8,128)S(1)}, bf16[192,12288]{1,0:T(8,128)(2,1)}, bf16[192,6144]{1,0:T(8,128)(2,1)}) custom-call(s32[1]{0:T(128)} %bitcast.core, s32[1]{0:T(128)} %bitcast.1.x, s32[1]{0:T(128)} %bitcast.2.z_lo, bf16[192,6144]{1,0:T(8,128)(2,1)S(1)} %take.2.own, ...), custom_call_target="tpu_custom_call" | custom-call | tf_op jit(solution)/shard_map/update/pallas_call | solution.py:203
  41.0 1.2 %collective-permute-done.14.theirs = f32[384,192]{1,0:T(8,128)S(1)} collective-permute-done((f32[384,192]{1,0:T(8,128)S(1)}, f32[384,192]{1,0:T(8,128)S(1)}, u32[]{:S(2)}, u32[]{:S(2)}) %collective-permute-start.14) | collective-permute-done | bytes 294944 | tf_op jit(solution)/shard_map/ppermute | solution.py:45
  42.2 2.9 %gradient.1 = bf16[64,144,128]{2,1,0:T(8,128)(2,1)} custom-call(f32[384,192]{1,0:T(8,128)S(1)} %get-tuple-element.13.mine, f32[384,192]{1,0:T(8,128)S(1)} %collective-permute-done.14.theirs, bf16[192,192]{1,0:T(8,128)(2,1)S(1)} %copy-done, bf16[192,192]{1,0:T(8,128)(2,1)S(1)} %collective-permute-done.12.signal_other, ...), custom_call_target="tpu_custom_call" | custom-call | tf_op jit(solution)/shard_map/gradient/pallas_call | solution.py:247
  45.1 6.9 %all-to-all-start = ((bf16[64,144,128]{2,1,0:T(8,128)(2,1)}), bf16[64,144,128]{2,1,0:T(8,128)(2,1)S(1)}, u32[]{:S(2)}, u32[]{:S(2)}) async-start(bf16[64,144,128]{2,1,0:T(8,128)(2,1)} %gradient.1), calls=%async_computation | async-start | bytes 4718592 | tf_op jit(solution)/shard_map/all_to_all | solution.py:344
  52.0 3.1 %place.1 = bf16[192,12288]{1,0:T(8,128)(2,1)} custom-call(s32[1]{0:T(128)} %bitcast.core, bf16[192,6144]{1,0:T(8,128)(2,1)} %collective-permute-done.13.fresh_back, bf16[192,12288]{1,0:T(8,128)(2,1)} %get-tuple-element.12.codes), custom_call_target="tpu_custom_call", output_to_operand_aliasing={{}: (2, {})} | custom-call | tf_op jit(solution)/shard_map/place/pallas_call | solution.py:271
  55.2 28.6 %all-to-all-done.pieces = bf16[64,144,128]{2,1,0:T(8,128)(2,1)S(1)} async-done(((bf16[64,144,128]{2,1,0:T(8,128)(2,1)}), bf16[64,144,128]{2,1,0:T(8,128)(2,1)S(1)}, u32[]{:S(2)}, u32[]{:S(2)}) %all-to-all-start) | async-done | bytes 2359328 | tf_op jit(solution)/shard_map/all_to_all | solution.py:344
  83.8 1.0 %finish.1 = f32[96,192]{1,0:T(8,128)} custom-call(bf16[64,144,128]{2,1,0:T(8,128)(2,1)S(1)} %all-to-all-done.pieces), custom_call_target="tpu_custom_call" | custom-call | tf_op jit(solution)/shard_map/finish/pallas_call | solution.py:295
  (24 shorter events, 1.3 us)
Async XLA Ops:
  0.6 3.2 %copy-start.1 = (bf16[768,192]{0,1:T(8,128)(2,1)S(1)}, bf16[768,192]{0,1:T(8,128)(2,1)}, u32[]{:S(2)}) copy-start(bf16[768,192]{0,1:T(8,128)(2,1)} %param.5) | copy-start | bytes 884740
  3.8 25.9 %collective-permute-start = (bf16[192,6144]{1,0:T(8,128)(2,1)}, bf16[192,6144]{1,0:T(8,128)(2,1)S(1)}, u32[]{:S(2)}, u32[]{:S(2)}) collective-permute-start(bf16[192,6144]{1,0:T(8,128)(2,1)} %take.3), channel_id=1, source_target_pairs={{0,8},{8,0},{1,9},{9,1},{2,10},{10,2},{3,11},{11,3},{4,12},{12,4},... | collective-permute-start | bytes 7077896 | tf_op jit(solution)/shard_map/ppermute | solution.py:45
  3.9 9.8 %collective-permute-start.2 = (bf16[192,768]{1,0:T(8,128)(2,1)S(1)}, bf16[192,768]{1,0:T(8,128)(2,1)S(1)}, u32[]{:S(2)}, u32[]{:S(2)}) collective-permute-start(bf16[192,768]{1,0:T(8,128)(2,1)S(1)} %bitcast.5), channel_id=1, source_target_pairs={{0,48},{16,0},{32,16},{48,32},{1,49},{17,1},{33,17},{49,33},{2,50}... | collective-permute-start | bytes 884744 | tf_op jit(solution)/shard_map/ppermute | solution.py:37
  6.8 10.6 %collective-permute-start.1 = (bf16[192,768]{1,0:T(8,128)(2,1)S(1)}, bf16[192,768]{1,0:T(8,128)(2,1)S(1)}, u32[]{:S(2)}, u32[]{:S(2)}) collective-permute-start(bf16[192,768]{1,0:T(8,128)(2,1)S(1)} %bitcast.6), channel_id=1, source_target_pairs={{0,16},{16,32},{32,48},{48,0},{1,17},{17,33},{33,49},{49,1},{2,18}... | collective-permute-start | bytes 884744 | tf_op jit(solution)/shard_map/ppermute | solution.py:37
  7.8 13.7 %collective-permute-start.3 = (bf16[96,768]{1,0:T(8,128)(2,1)S(1)}, bf16[96,768]{1,0:T(8,128)(2,1)S(1)}, u32[]{:S(2)}, u32[]{:S(2)}) collective-permute-start(bf16[96,768]{1,0:T(8,128)(2,1)S(1)} %get-tuple-element.9.refs_0_), channel_id=1, source_target_pairs={{0,64},{64,4},{4,68},{68,0},{1,65},{65,5},{5,69},{69,1},{2,66},{66... | collective-permute-start | bytes 442376 | tf_op jit(solution)/shard_map/ppermute | solution.py:41
  9.8 11.8 %collective-permute-start.4 = (bf16[96,768]{1,0:T(8,128)(2,1)S(1)}, bf16[96,768]{1,0:T(8,128)(2,1)S(1)}, u32[]{:S(2)}, u32[]{:S(2)}) collective-permute-start(bf16[96,768]{1,0:T(8,128)(2,1)S(1)} %get-tuple-element.10.refs_1_), channel_id=1, source_target_pairs={{0,68},{64,0},{4,64},{68,4},{1,69},{65,1},{5,65},{69,5},{2,70},{66... | collective-permute-start | bytes 442376 | tf_op jit(solution)/shard_map/ppermute | solution.py:41
  13.7 8.0 %collective-permute-start.6 = (bf16[96,768]{1,0:T(8,128)(2,1)S(1)}, bf16[96,768]{1,0:T(8,128)(2,1)S(1)}, u32[]{:S(2)}, u32[]{:S(2)}) collective-permute-start(bf16[96,768]{1,0:T(8,128)(2,1)S(1)} %slice.9), channel_id=1, source_target_pairs={{0,48},{16,0},{32,16},{48,32},{1,49},{17,1},{33,17},{49,33},{2,50}... | collective-permute-start | bytes 442376 | tf_op jit(solution)/shard_map/ppermute | solution.py:37
  17.4 13.1 %collective-permute-start.8 = (bf16[192,768]{1,0:T(8,128)(2,1)S(1)}, bf16[192,768]{1,0:T(8,128)(2,1)S(1)}, u32[]{:S(2)}, u32[]{:S(2)}) collective-permute-start(bf16[192,768]{1,0:T(8,128)(2,1)S(1)} %collective-permute-done.2.refs_3_), channel_id=1, source_target_pairs={{0,68},{64,0},{4,64},{68,4},{1,69},{65,1},{5,65},{69,5},{2,70},{66... | collective-permute-start | bytes 884744 | tf_op jit(solution)/shard_map/ppermute | solution.py:41
  21.5 10.0 %collective-permute-start.7 = (bf16[192,768]{1,0:T(8,128)(2,1)S(1)}, bf16[192,768]{1,0:T(8,128)(2,1)S(1)}, u32[]{:S(2)}, u32[]{:S(2)}) collective-permute-start(bf16[192,768]{1,0:T(8,128)(2,1)S(1)} %collective-permute-done.1.refs_2_), channel_id=1, source_target_pairs={{0,64},{64,4},{4,68},{68,0},{1,65},{65,5},{5,69},{69,1},{2,66},{66... | collective-permute-start | bytes 884744 | tf_op jit(solution)/shard_map/ppermute | solution.py:41
  21.6 6.4 %collective-permute-start.5 = (bf16[96,768]{1,0:T(8,128)(2,1)S(1)}, bf16[96,768]{1,0:T(8,128)(2,1)S(1)}, u32[]{:S(2)}, u32[]{:S(2)}) collective-permute-start(bf16[96,768]{1,0:T(8,128)(2,1)S(1)} %slice.8), channel_id=1, source_target_pairs={{0,16},{16,32},{32,48},{48,0},{1,17},{17,33},{33,49},{49,1},{2,18}... | collective-permute-start | bytes 442376 | tf_op jit(solution)/shard_map/ppermute | solution.py:37
  21.7 10.5 %collective-permute-start.10 = (bf16[96,768]{1,0:T(8,128)(2,1)S(1)}, bf16[96,768]{1,0:T(8,128)(2,1)S(1)}, u32[]{:S(2)}, u32[]{:S(2)}) collective-permute-start(bf16[96,768]{1,0:T(8,128)(2,1)S(1)} %collective-permute-done.6.refs_2_.refs_7_), channel_id=1, source_target_pairs={{0,68},{64,0},{4,64},{68,4},{1,69},{65,1},{5,65},{69,5},{2,70},{66... | collective-permute-start | bytes 442376 | tf_op jit(solution)/shard_map/ppermute | solution.py:41
  28.0 6.4 %collective-permute-start.9 = (bf16[96,768]{1,0:T(8,128)(2,1)S(1)}, bf16[96,768]{1,0:T(8,128)(2,1)S(1)}, u32[]{:S(2)}, u32[]{:S(2)}) collective-permute-start(bf16[96,768]{1,0:T(8,128)(2,1)S(1)} %collective-permute-done.5.refs_1_.refs_6_), channel_id=1, source_target_pairs={{0,64},{64,4},{4,68},{68,0},{1,65},{65,5},{5,69},{69,1},{2,66},{66... | collective-permute-start | bytes 442376 | tf_op jit(solution)/shard_map/ppermute | solution.py:41
  32.2 2.6 %copy-start = (bf16[192,192]{1,0:T(8,128)(2,1)S(1)}, bf16[192,192]{1,0:T(8,128)(2,1)}, u32[]{:S(2)}) copy-start(bf16[192,192]{1,0:T(8,128)(2,1)} %signal_own.3) | copy-start | bytes 221188
  34.7 1.9 %collective-permute-start.11 = (f32[384,192]{1,0:T(8,128)S(1)}, f32[384,192]{1,0:T(8,128)S(1)}, u32[]{:S(2)}, u32[]{:S(2)}) collective-permute-start(f32[384,192]{1,0:T(8,128)S(1)} %estimate.5.mine), channel_id=1, source_target_pairs={{0,8},{8,0},{1,9},{9,1},{2,10},{10,2},{3,11},{11,3},{4,12},{12,4},... | collective-permute-start | bytes 884744 | tf_op jit(solution)/shard_map/ppermute | solution.py:45
  34.8 1.8 %collective-permute-start.12 = (bf16[192,192]{1,0:T(8,128)(2,1)S(1)}, bf16[192,192]{1,0:T(8,128)(2,1)S(1)}, u32[]{:S(2)}, u32[]{:S(2)}) collective-permute-start(bf16[192,192]{1,0:T(8,128)(2,1)S(1)} %copy-done), channel_id=1, source_target_pairs={{0,8},{8,0},{1,9},{9,1},{2,10},{10,2},{3,11},{11,3},{4,12},{12,4},... | collective-permute-start | bytes 221192 | tf_op jit(solution)/shard_map/ppermute | solution.py:45
  40.4 1.8 %collective-permute-start.14 = (f32[384,192]{1,0:T(8,128)S(1)}, f32[384,192]{1,0:T(8,128)S(1)}, u32[]{:S(2)}, u32[]{:S(2)}) collective-permute-start(f32[384,192]{1,0:T(8,128)S(1)} %get-tuple-element.13.mine), channel_id=1, source_target_pairs={{0,8},{8,0},{1,9},{9,1},{2,10},{10,2},{3,11},{11,3},{4,12},{12,4},... | collective-permute-start | bytes 884744 | tf_op jit(solution)/shard_map/ppermute | solution.py:45
  40.6 11.4 %collective-permute-start.13 = (bf16[192,6144]{1,0:T(8,128)(2,1)}, bf16[192,6144]{1,0:T(8,128)(2,1)}, u32[]{:S(2)}, u32[]{:S(2)}) collective-permute-start(bf16[192,6144]{1,0:T(8,128)(2,1)} %get-tuple-element.11), channel_id=1, source_target_pairs={{0,8},{8,0},{1,9},{9,1},{2,10},{10,2},{3,11},{11,3},{4,12},{12,4},... | collective-permute-start | bytes 7077896 | tf_op jit(solution)/shard_map/ppermute | solution.py:45
  45.1 38.6 %all-to-all-start = ((bf16[64,144,128]{2,1,0:T(8,128)(2,1)}), bf16[64,144,128]{2,1,0:T(8,128)(2,1)S(1)}, u32[]{:S(2)}, u32[]{:S(2)}) async-start(bf16[64,144,128]{2,1,0:T(8,128)(2,1)} %gradient.1), calls=%async_computation | async-start | bytes 4718592 | tf_op jit(solution)/shard_map/all_to_all | solution.py:344
